TPU v7x, 512 devices: a whole 4x4x16 slice. The times are simulated.
512 devices in a mesh: seg: 32 (over z_lo, y), blk: 16 (over z_hi, x, core).
Axes of the slice: x: 4, y: 4, z: 16 (z_hi: 2, z_lo: 8; z = z_hi * 8 + z_lo), core: 2. Of those that a mesh axis runs over, the one named last changes fastest.
Arguments:
- queries: float32 [65536, 1024], P(('seg', 'blk')), may hold values from -5 to 5
- keys: float32 [65536, 256], P(('seg', 'blk')), may hold values from -5 to 5
- values: float32 [65536, 256], P(('seg', 'blk')), may hold values from -6 to 6
- gate_logit: float32 [8], replicated, may hold values from -3 to 3
- memory_gain: float32 [1024], replicated, may hold values from 0.5 to 2
Outputs:
- mixed: float32 [65536, 1024], P(('seg', 'blk'))
All inputs are finite; a program needn't handle non-finite values.
Results may differ from a plain program's by a relative error of at most 0.0003.
Values sent between devices are 32-bit elements; how exact they have to be, the bound alone decides.
A program may use at most 64 MiB of HBM per device.

v0:
```python
import jax
import jax.numpy as jnp
from jax import lax
from jax.sharding import PartitionSpec as P

QH = 8
KVH = 2
GROUP = 4
HD = 128
HIGH = lax.Precision.HIGHEST


def side_by_side(arrays, axis, dim, along):
    widths = [a.shape[along] for a in arrays]
    both = jnp.concatenate(arrays, axis=along)
    filled = lax.all_gather(both, axis, axis=dim, tiled=True)
    return tuple(jnp.split(filled, [sum(widths[:k]) for k in range(1, len(widths))], axis=along))


def split_up(shard, dim, peers):
    before, after = (shard.shape[:dim], shard.shape[dim + 1 :])
    return jnp.moveaxis(shard.reshape(*before, peers, -1, *after), dim, 0)


def sent_and_summed(shard, axis, dim):
    peers = lax.axis_size(axis)
    parts = lax.all_to_all(split_up(shard, dim, peers), axis, 0, 0, tiled=True)
    return jnp.sum(parts, axis=0)


def from_everyone(shard, axis):
    copies = jnp.broadcast_to(shard, (lax.axis_size(axis), *shard.shape))
    return lax.all_to_all(copies, axis, split_axis=0, concat_axis=0, tiled=True)


def joined_by_halves(pieces, combine):
    while len(jax.tree.leaves(pieces)[0]) > 1:
        pieces = jax.vmap(combine)(*(pieces[side::2] for side in (0, 1)))
    return pieces[0]


def carried_in(shard, axis, combine, identity):
    peers, index = (lax.axis_size(axis), lax.axis_index(axis))
    passed = jnp.arange(peers) < index

    def kept(part, zero, own):
        part = jnp.where(
            passed.reshape(-1, *(1 for _ in own.shape)), part, jnp.asarray(zero, own.dtype)
        )
        return part

    pieces = from_everyone(shard, axis)
    return joined_by_halves(kept(pieces, identity, shard), combine)


def sigma_map(x):
    return jnp.where(x > 0, x + 1.0, jnp.exp(jnp.minimum(x, 0.0)))


def add_terms(earlier, later):
    return earlier + later


def on_device(queries, keys, values, gate_logit, memory_gain):
    rows = queries.shape[0]
    index = lax.axis_index("blk")
    q_heads = queries.reshape(rows, KVH, GROUP, HD)
    qpos = index * rows + jnp.arange(rows, dtype=jnp.int32)
    scale = 1.0 / jnp.sqrt(jnp.float32(HD))

    def update(carry, pieces):
        top, total, accum = carry
        k_piece, v_piece = pieces
        count = k_piece.shape[0]
        k_h = k_piece.reshape(count, KVH, HD)
        v_h = v_piece.reshape(count, KVH, HD)
        scores = jnp.einsum("rkgd,nkd->kgrn", q_heads, k_h, precision=HIGH) * scale
        kpos = jnp.arange(count, dtype=jnp.int32)
        allowed = (kpos[None, :] <= qpos[:, None])[None, None]
        row_top = jnp.max(jnp.where(allowed, scores, -1e30), axis=-1)
        new_top = jnp.maximum(top, row_top)
        weights = jnp.where(allowed, jnp.exp(scores - new_top[..., None]), 0.0)
        total = jnp.sum(weights, axis=-1)
        accum = jnp.einsum("kgrn,nkd->kgrd", weights, v_h, precision=HIGH)
        return (new_top, total, accum)

    start_state = (
        jnp.full((KVH, GROUP, rows), -1e30, jnp.float32),
        jnp.zeros((KVH, GROUP, rows), jnp.float32),
        jnp.zeros((KVH, GROUP, rows, HD), jnp.float32),
    )
    pieces = side_by_side((keys, values), "blk", 0, 1)
    top, total, accum = lax.cond(
        jnp.int32(0) <= qpos[rows - 1], lambda c: update(c, pieces), lambda c: c, start_state
    )
    attention = accum / total[..., None]
    sig_keys = sigma_map(keys.reshape(rows, KVH, HD))
    partial_value = jnp.einsum(
        "rkd,rke->kde", sig_keys, values.reshape(rows, KVH, HD), precision=HIGH
    ).reshape(KVH * HD, HD)
    shard = sent_and_summed(partial_value, "blk", 0)
    prefix = carried_in(shard, "seg", add_terms, jnp.zeros_like(shard))
    memory = lax.all_gather(prefix, "blk", axis=0, tiled=True)
    retrieval = jnp.einsum(
        "rkgd,kde->kgre", sigma_map(q_heads), memory.reshape(KVH, HD, HD), precision=HIGH
    )
    rms = jnp.sqrt(jnp.mean(retrieval * retrieval, axis=-1, keepdims=True) + 1e-06)
    normed = retrieval / rms * memory_gain.reshape(KVH, GROUP, 1, HD)
    gate = jax.nn.sigmoid(gate_logit).reshape(KVH, GROUP, 1, 1)
    mixed = gate * normed + (1.0 - gate) * attention
    return jnp.transpose(mixed, (2, 0, 1, 3)).reshape(rows, QH * HD)


def solution(mesh):
    return jax.shard_map(
        on_device,
        mesh=mesh,
        in_specs=(
            P(("seg", "blk"), None),
            P(("seg", "blk"), None),
            P(("seg", "blk"), None),
            P(),
            P(),
        ),
        out_specs=P(("seg", "blk"), None),
        check_vma=False,
    )
```

profile of v0, /device:TPU:3, one launch (start us, length us, event | category | flops | bytes accessed | tf_op | source)
XLA Modules:
  0.0 169.8 jit_solution(6998863623988860291)
XLA Ops:
  6.5 0.0 all-gather.3.cloned.1.call-start
  6.5 1.0 copy.19
  7.5 1.0 copy.20
  8.5 0.7 pad_maximum_fusion
  9.3 0.0 all-gather.3.cloned.1.call-update
  9.3 0.9 exponential_select_fusion
  10.2 0.1 copy.34
  10.3 1.2 fusion.19
  11.5 32.2 %all_to_all.10 = f32[16,16,128]{2,1,0:T(8,128)S(1)} all-to-all(f32[16,16,128]{2,1,0:T(8,128)S(1)} %bitcast.56), channel_id=1, replica_groups=mesh['seg'=32,'blk'=16] {'blk'}, dimensions={0} | all-to-all | bytes 262144 | tf_op jit(solution)/shard_map/all_to_all | solution.py:27
  43.8 0.7 broadcast_in_dim.50
  44.5 16.2 %all-to-all-start.1 = ((f32[32,16,128]{2,1,0:T(8,128)}), f32[32,16,128]{2,1,0:T(8,128)S(1)}, u32[]{:S(2)}, u32[]{:S(2)}) async-start(f32[32,16,128]{2,1,0:T(8,128)} %broadcast_in_dim.50), calls=%async_computation.1 | async-start | bytes 524288 | tf_op jit(solution)/shard_map/all_to_all | solution.py:33
  60.7 1.2 copy.16
  61.9 0.6 slice.45
  63.1 0.7 add_divide_fusion
  63.8 0.1 mul.40
  63.9 10.7 %all-to-all-done.1 = f32[32,16,128]{2,1,0:T(8,128)S(1)} async-done(((f32[32,16,128]{2,1,0:T(8,128)}), f32[32,16,128]{2,1,0:T(8,128)S(1)}, u32[]{:S(2)}, u32[]{:S(2)}) %all-to-all-start.1) | async-done | bytes 262176 | tf_op jit(solution)/shard_map/all_to_all | solution.py:33
  74.5 0.1 broadcast_select_fusion
  74.7 59.1 %all-gather = f32[1,256,128]{2,1,0:T(8,128)S(1)} all-gather(f32[1,16,128]{2,1,0:T(8,128)S(1)} %slice_add_fusion.4), channel_id=2, replica_groups=mesh['seg'=32,'blk'=16] {'blk'}, dimensions={1}, use_global_device_ids=true | all-gather | bytes 139264 | tf_op jit(solution)/shard_map/all_gather | solution.py:103
  133.9 0.7 multiply_reduce_fusion
  134.6 8.6 %all-gather.3.cloned.1.call-done = f32[2048,512]{0,1:T(8,128)} async-done(((f32[128,512]{0,1:T(8,128)}), f32[2048,512]{0,1:T(8,128)}) %all-gather.3.cloned.1.call-update) | async-done | bytes 4194320 | tf_op jit(solution)/shard_map/all_gather | solution.py:16
  143.2 0.0 copy-start
  143.2 18.4 %conditional.1 = (f32[2,4,128]{2,1,0:T(4,128)S(1)}, f32[2,4,128,128]{2,3,1,0:T(8,128)S(1)}) conditional(s32[]{:T(128)} %bitcast.12, () %tuple.13, (s32[128]{0:T(128)S(1)}, f32[2048,512]{0,1:T(8,128)}, f32[128,2,4,128]{0,3,2,1:T(8,128)S(1)}) %tuple.25), branch_computations={%region_2.0_spmd, %region_3.6_spmd} | conditional | flops 6463683584 | bytes 39870992 | solution.py:93
  143.2 0.2 iota_compare_fusion
  143.4 2.5 %fusion.24 = (f32[2048,256]{0,1:T(8,128)S(1)}, f32[2048,256]{0,1:T(8,128)S(1)}) fusion(f32[2048,512]{0,1:T(8,128)} %get-tuple-element.15), kind=kLoop, calls=%fused_computation.43 | loop fusion | bytes 8388608 | tf_op jit(solution)/shard_map/split | solution.py:17
  145.9 7.3 %fusion = (f32[2,4,128]{2,1,0:T(4,128)S(1)}, f32[2,2048,128,4]{2,1,3,0:T(8,128)S(1)}) fusion(pred[128,2048]{0,1:T(8,128)(4,1)S(1)} %iota_compare_fusion, f32[2048,2,128,1]{0,2,3,1:T(8,128)S(1)} %bitcast.49, f32[128,2,4,128]{0,3,2,1:T(8,128)S(1)} %get-tuple-element.23), kind=kOutput, calls=%fused_computation.2 | convolution fusion | flops 3227515904 | bytes 11276288 | tf_op jit(solution)/shard_map/cond/branch_1_fun/rkgd,nkd->kgrn/dot_general | solution.py:77
  153.2 6.4 %fusion.3 = f32[2,4,128,128]{2,3,1,0:T(8,128)S(1)} fusion(f32[2048,2,128,1]{0,2,3,1:T(8,128)S(1)} %bitcast.53, f32[2,2048,128,4]{2,1,3,0:T(8,128)S(1)} %get-tuple-element.28, f32[2,4,128]{2,1,0:T(4,128)S(1)} %broadcast_maximum_fusion, pred[128,2048]{0,1:T(8,128)(4,1)S(1)} %iota_compare_fusion), kind=kOutput, calls=%fused_computation.5 | convolution fusion | flops 3227516928 | bytes 11276288 | tf_op jit(solution)/shard_map/cond | solution.py:93
  159.7 1.7 %fusion.5 = f32[2,4,128]{2,1,0:T(4,128)S(1)} fusion(f32[2,2048,128,4]{2,1,3,0:T(8,128)S(1)} %get-tuple-element.28, f32[2,4,128]{2,1,0:T(4,128)S(1)} %broadcast_maximum_fusion, pred[128,2048]{0,1:T(8,128)(4,1)S(1)} %iota_compare_fusion), kind=kLoop, calls=%fused_computation.6 | loop fusion | flops 8387584 | bytes 8658944 | tf_op jit(solution)/shard_map/cond/branch_1_fun/reduce_sum | solution.py:83
  161.7 0.0 copy-done
  161.7 0.2 multiply_add_fusion
  161.9 1.0 copy.23
  (11 shorter events, 0.1 us)
Async XLA Ops:
  6.5 136.7 %all-gather.3.cloned.1.call-start = ((), (), s32[]{:S(2)}) async-start(), calls=%async_computation.2 | async-start | bytes 4456448 | tf_op jit(solution)/shard_map/all_gather | solution.py:16
  44.5 30.1 %all-to-all-start.1 = ((f32[32,16,128]{2,1,0:T(8,128)}), f32[32,16,128]{2,1,0:T(8,128)S(1)}, u32[]{:S(2)}, u32[]{:S(2)}) async-start(f32[32,16,128]{2,1,0:T(8,128)} %broadcast_in_dim.50), calls=%async_computation.1 | async-start | bytes 524288 | tf_op jit(solution)/shard_map/all_to_all | solution.py:33
  143.2 18.5 %copy-start = (f32[1024]{0:T(1024)S(1)}, f32[1024]{0:T(1024)}, u32[]{:S(2)}) copy-start(f32[1024]{0:T(1024)} %param.11) | copy-start | bytes 12292
Sparse Core Ops, SparseCore 0:
  10.5 132.6 all-gather.2
where the time goes:
time: 170 us
  blocking collectives  91.4 us (54%)
  waiting for transfers between devices  19.3 us (11%)
  starting transfers between devices  16.2 us (10%)
  matrix products  15.6 us (9%)
  between operations  14.1 us (8%)
  local copies, waits for them, and re-layouts  8.18 us (5%)
  other arithmetic  4.63 us (3%)
    all_gather x1, blocking collectives, on_device(): memory = lax.all_gather(prefix, 'blk', axis=0, tiled=True)  59.1 us
    all_to_all x1, blocking collectives, sent_and_summed(): parts = lax.all_to_all(split_up(shard, dim, peers), axis, 0, 0, tiled=True)  32.2 us
    all_to_all x1, starting transfers between devices, from_everyone(): return lax.all_to_all(copies, axis, split_axis=0, concat_axis=0, tiled=True)  16.2 us
    all_to_all x1, waiting for transfers between devices, from_everyone(): return lax.all_to_all(copies, axis, split_axis=0, concat_axis=0, tiled=True)  10.7 us
    all_gather x1, waiting for transfers between devices, side_by_side(): filled = lax.all_gather(both, axis, axis=dim, tiled=True)  8.63 us
    dot_general x1, matrix products, update(): scores = jnp.einsum('rkgd,nkd->kgrn', q_heads, k_h, precision=HIGH) * scale  7.34 us
    cond x1, matrix products, on_device(): lax.cond(jnp.int32(0) <= qpos[rows - 1], lambda c: update(c, pieces), lam...  6.44 us
  transfers between devices with their start and end apart: 2, of which 2 were waited for; matrix products, arithmetic and copies ran while one was open for 4% of the time, Pallas kernels for 0%

commit v1 on v0

--- a/solution.py
+++ b/solution.py
@@ -100,7 +100,8 @@
     ).reshape(KVH * HD, HD)
     shard = sent_and_summed(partial_value, "blk", 0)
     prefix = carried_in(shard, "seg", add_terms, jnp.zeros_like(shard))
-    memory = lax.all_gather(prefix, "blk", axis=0, tiled=True)
+    outgoing = jnp.stack([prefix] * lax.axis_size("blk"))
+    memory = jnp.concatenate(lax.all_to_all(outgoing, "blk", 0, 0), axis=0)
     retrieval = jnp.einsum(
         "rkgd,kde->kgre", sigma_map(q_heads), memory.reshape(KVH, HD, HD), precision=HIGH
     )

time: 170 us -> 172 us (1.012)
  the two profiles are of different devices: /device:TPU:3 before, /device:TPU:1 now
where the time goes in v1:
time: 172 us
  waiting for transfers between devices  71.9 us (42%)
  blocking collectives  34 us (20%)
  starting transfers between devices  22.6 us (13%)
  matrix products  15.6 us (9%)
  between operations  14.1 us (8%)
  local copies, waits for them, and re-layouts  8.83 us (5%)
  other arithmetic  4.63 us (3%)
    all_gather x1, waiting for transfers between devices, side_by_side(): filled = lax.all_gather(both, axis, axis=dim, tiled=True)  38 us
    all_to_all x1, blocking collectives, sent_and_summed(): parts = lax.all_to_all(split_up(shard, dim, peers), axis, 0, 0, tiled=True)  34 us
    all_to_all x1, waiting for transfers between devices, on_device(): memory = jnp.concatenate(lax.all_to_all(outgoing, 'blk', 0, 0), axis=0)  20.1 us
    all_to_all x1, waiting for transfers between devices, from_everyone(): return lax.all_to_all(copies, axis, split_axis=0, concat_axis=0, tiled=True)  13.8 us
    all_to_all x1, starting transfers between devices, from_everyone(): return lax.all_to_all(copies, axis, split_axis=0, concat_axis=0, tiled=True)  12.2 us
    all_to_all x1, starting transfers between devices, on_device(): memory = jnp.concatenate(lax.all_to_all(outgoing, 'blk', 0, 0), axis=0)  10.4 us
    dot_general x1, matrix products, update(): scores = jnp.einsum('rkgd,nkd->kgrn', q_heads, k_h, precision=HIGH) * scale  7.34 us
    cond x1, matrix products, on_device(): lax.cond(jnp.int32(0) <= qpos[rows - 1], lambda c: update(c, pieces), lam...  6.44 us
  transfers between devices with their start and end apart: 3, of which 3 were waited for; matrix products, arithmetic and copies ran while one was open for 4% of the time, Pallas kernels for 0%

profile of v1, /device:TPU:1, one launch (start us, length us, event | category | flops | bytes accessed | tf_op | source)
XLA Modules:
  0.0 172.0 jit_solution(13924990070404770850)
XLA Ops:
  6.5 0.0 all-gather.2.cloned.1.call-start
  6.5 1.0 copy.19
  7.5 1.0 copy.20
  8.5 0.7 pad_maximum_fusion
  9.3 0.0 all-gather.2.cloned.1.call-update
  9.3 0.9 exponential_select_fusion
  10.2 0.1 copy.34
  10.3 1.2 fusion.19
  11.5 34.0 %all_to_all.15 = f32[16,16,128]{2,1,0:T(8,128)S(1)} all-to-all(f32[16,16,128]{2,1,0:T(8,128)S(1)} %bitcast.58), channel_id=1, replica_groups=mesh['seg'=32,'blk'=16] {'blk'}, dimensions={0} | all-to-all | bytes 262144 | tf_op jit(solution)/shard_map/all_to_all | solution.py:27
  45.6 0.7 broadcast_in_dim.50
  46.3 12.2 %all-to-all-start.1 = ((f32[32,16,128]{2,1,0:T(8,128)}), f32[32,16,128]{2,1,0:T(8,128)S(1)}, u32[]{:S(2)}, u32[]{:S(2)}) async-start(f32[32,16,128]{2,1,0:T(8,128)} %broadcast_in_dim.50), calls=%async_computation.1 | async-start | bytes 524288 | tf_op jit(solution)/shard_map/all_to_all | solution.py:33
  58.5 13.8 %all-to-all-done.1 = f32[32,16,128]{2,1,0:T(8,128)S(1)} async-done(((f32[32,16,128]{2,1,0:T(8,128)}), f32[32,16,128]{2,1,0:T(8,128)S(1)}, u32[]{:S(2)}, u32[]{:S(2)}) %all-to-all-start.1) | async-done | bytes 262176 | tf_op jit(solution)/shard_map/all_to_all | solution.py:33
  72.3 0.1 broadcast_select_fusion
  72.5 0.7 stack.3
  73.1 10.4 %all-to-all-start.2 = ((f32[16,16,128]{2,1,0:T(8,128)}), f32[16,16,128]{2,1,0:T(8,128)S(1)}, u32[]{:S(2)}, u32[]{:S(2)}) async-start(f32[16,16,128]{2,1,0:T(8,128)} %stack.3), calls=%async_computation.2 | async-start | bytes 262144 | tf_op jit(solution)/shard_map/all_to_all | solution.py:104
  83.6 1.2 copy.16
  84.8 0.6 slice.45
  85.9 0.7 add_divide_fusion
  86.6 0.1 mul.40
  86.7 20.1 %all-to-all-done.2 = f32[16,16,128]{2,1,0:T(8,128)S(1)} async-done(((f32[16,16,128]{2,1,0:T(8,128)}), f32[16,16,128]{2,1,0:T(8,128)S(1)}, u32[]{:S(2)}, u32[]{:S(2)}) %all-to-all-start.2) | async-done | bytes 131104 | tf_op jit(solution)/shard_map/all_to_all | solution.py:104
  106.8 0.7 multiply_reduce_fusion
  107.5 38.0 %all-gather.2.cloned.1.call-done = f32[2048,512]{0,1:T(8,128)} async-done(((f32[128,512]{0,1:T(8,128)}), f32[2048,512]{0,1:T(8,128)}) %all-gather.2.cloned.1.call-update) | async-done | bytes 4194320 | tf_op jit(solution)/shard_map/all_gather | solution.py:16
  145.5 0.0 copy-start
  145.5 18.4 %conditional.1 = (f32[2,4,128]{2,1,0:T(4,128)S(1)}, f32[2,4,128,128]{2,3,1,0:T(8,128)S(1)}) conditional(s32[]{:T(128)} %bitcast.13, () %tuple.13, (s32[128]{0:T(128)S(1)}, f32[2048,512]{0,1:T(8,128)}, f32[128,2,4,128]{0,3,2,1:T(8,128)S(1)}) %tuple.25), branch_computations={%region_2.0_spmd, %region_3.6_spmd} | conditional | flops 6463683584 | bytes 39870992 | solution.py:93
  145.5 0.2 iota_compare_fusion
  145.7 2.5 %fusion.25 = (f32[2048,256]{0,1:T(8,128)S(1)}, f32[2048,256]{0,1:T(8,128)S(1)}) fusion(f32[2048,512]{0,1:T(8,128)} %get-tuple-element.15), kind=kLoop, calls=%fused_computation.44 | loop fusion | bytes 8388608 | tf_op jit(solution)/shard_map/split | solution.py:17
  148.2 7.3 %fusion = (f32[2,4,128]{2,1,0:T(4,128)S(1)}, f32[2,2048,128,4]{2,1,3,0:T(8,128)S(1)}) fusion(pred[128,2048]{0,1:T(8,128)(4,1)S(1)} %iota_compare_fusion, f32[2048,2,128,1]{0,2,3,1:T(8,128)S(1)} %bitcast.51, f32[128,2,4,128]{0,3,2,1:T(8,128)S(1)} %get-tuple-element.23), kind=kOutput, calls=%fused_computation.2 | convolution fusion | flops 3227515904 | bytes 11276288 | tf_op jit(solution)/shard_map/cond/branch_1_fun/rkgd,nkd->kgrn/dot_general | solution.py:77
  155.5 6.4 %fusion.3 = f32[2,4,128,128]{2,3,1,0:T(8,128)S(1)} fusion(f32[2048,2,128,1]{0,2,3,1:T(8,128)S(1)} %bitcast.55, f32[2,2048,128,4]{2,1,3,0:T(8,128)S(1)} %get-tuple-element.28, f32[2,4,128]{2,1,0:T(4,128)S(1)} %broadcast_maximum_fusion, pred[128,2048]{0,1:T(8,128)(4,1)S(1)} %iota_compare_fusion), kind=kOutput, calls=%fused_computation.5 | convolution fusion | flops 3227516928 | bytes 11276288 | tf_op jit(solution)/shard_map/cond | solution.py:93
  162.0 1.7 fusion.5
  163.9 0.0 copy-done
  164.0 0.2 multiply_add_fusion
  164.2 1.0 copy.23
  (11 shorter events, 0.1 us)
Async XLA Ops:
  6.5 139.0 %all-gather.2.cloned.1.call-start = ((), (), s32[]{:S(2)}) async-start(), calls=%async_computation.3 | async-start | bytes 4456448 | tf_op jit(solution)/shard_map/all_gather | solution.py:16
  46.3 26.0 %all-to-all-start.1 = ((f32[32,16,128]{2,1,0:T(8,128)}), f32[32,16,128]{2,1,0:T(8,128)S(1)}, u32[]{:S(2)}, u32[]{:S(2)}) async-start(f32[32,16,128]{2,1,0:T(8,128)} %broadcast_in_dim.50), calls=%async_computation.1 | async-start | bytes 524288 | tf_op jit(solution)/shard_map/all_to_all | solution.py:33
  73.1 33.6 %all-to-all-start.2 = ((f32[16,16,128]{2,1,0:T(8,128)}), f32[16,16,128]{2,1,0:T(8,128)S(1)}, u32[]{:S(2)}, u32[]{:S(2)}) async-start(f32[16,16,128]{2,1,0:T(8,128)} %stack.3), calls=%async_computation.2 | async-start | bytes 262144 | tf_op jit(solution)/shard_map/all_to_all | solution.py:104
  145.5 18.5 %copy-start = (f32[1024]{0:T(1024)S(1)}, f32[1024]{0:T(1024)}, u32[]{:S(2)}) copy-start(f32[1024]{0:T(1024)} %param.11) | copy-start | bytes 12292
Sparse Core Ops, SparseCore 0:
  10.5 134.9 all-gather.1
